TPU v7x, 32 devices: a whole 2x2x4 slice. The times are simulated.
32 devices in a mesh: frames: 2 (over x), lenslet: 16 (over z, y, core).
Axes of the slice: x: 2, y: 2, z: 4, core: 2. Of those that a mesh axis runs over, the one named last changes fastest.
Arguments:
- volume: bfloat16 [8, 256, 64, 400], P('frames', 'lenslet'), parts along dimension 0, may hold values from 0.099609375 to 1
- measured: float32 [512, 64, 400], P(('frames', 'lenslet')), parts along dimension 0, may hold values from 0.2 to 2
- operator_rows: bfloat16 [12800, 400], P('lenslet'), may hold values from 2.9831426e-10 to 0.0029907227
- offset_counts: int32 [4], replicated, may hold values from 1 to 25, 32 in all
- offset_table: int32 [32, 2], replicated, may hold values from -2 to 2
- dark_level: float32 [400], replicated, may hold values from 0.2 to 1
Outputs:
- predicted: float32 [512, 64, 400], P(('frames', 'lenslet')), parts along dimension 0
- ratio: float32 [512, 64, 400], P(('frames', 'lenslet')), parts along dimension 0
There are 2 independent parts, one for each index of `frames`. A program takes and returns all parts, laid end to end along the dimension named above; an argument that names none is the same for every part. Nothing has to cross between parts.
Inputs may be any that keep to these rules, and one draw needn't show every extreme that they name: `offset_counts`: counts sum to 32.
All inputs are finite; a program needn't handle non-finite values.
Results may differ from a plain program's by a relative error of at most 0.0003.
Values may be sent and summed in bfloat16 or wider, within the bound.
No kernel may reach another device: no remote copies, remote signals or barrier semaphores. Data moves between devices by JAX's collectives and lax.ppermute only.
A program may use at most 192 MiB of HBM per device.

v0:
```python
import jax
import jax.numpy as jnp
from jax import lax
from jax.sharding import PartitionSpec as P

REACH = 2


def passed_along(block, axis, distance):
    devices = range(lax.axis_size(axis))
    route = [(i - distance, i) for i in devices if i - distance in devices]
    return lax.ppermute(block, axis, route)


def gather_slabs(table, depth_of, row_start, col_shift, target_rows, columns, rows_ext, cols_ext):
    row_ids = jnp.arange(target_rows, dtype=jnp.int32)
    col_ids = jnp.arange(columns, dtype=jnp.int32)
    index = depth_of[None, None, :] * (rows_ext * cols_ext)
    index = index + (row_ids[:, None, None] + row_start[None, None, :]) * cols_ext
    index = index + col_ids[None, :, None] + col_shift[None, None, :] + REACH
    pixels = table.shape[1]
    taken = jnp.take(table, index.reshape(-1), axis=0)
    return taken.reshape(target_rows * columns, depth_of.shape[0] * pixels)


def body(volume, measured, operator_rows, offset_counts, offset_table, dark_level):
    depths, rows_here, columns, pixels = volume.shape
    op_total = offset_table.shape[0]
    ends = jnp.cumsum(offset_counts)
    positions = jnp.arange(op_total, dtype=jnp.int32)
    depth_of = jnp.sum((positions[:, None] >= ends[None, :]).astype(jnp.int32), axis=1)
    row_shift = offset_table[:, 0]
    col_shift = offset_table[:, 1]
    cols_ext = columns + 2 * REACH
    above = passed_along(volume[:, rows_here - REACH :], "lenslet", 1)
    below = passed_along(volume[:, :REACH], "lenslet", -1)
    extended = jnp.concatenate([above, volume, below], axis=1)
    extended = jnp.pad(extended, ((0, 0), (0, 0), (REACH, REACH), (0, 0)))
    rows_ext = rows_here + 2 * REACH
    table = extended.reshape(depths * rows_ext * cols_ext, pixels)
    stacked = gather_slabs(
        table, depth_of, row_shift + REACH, col_shift, rows_here, columns, rows_ext, cols_ext
    )
    summed = jnp.dot(
        stacked,
        lax.all_gather(operator_rows, "lenslet", axis=0, tiled=True),
        preferred_element_type=jnp.float32,
    )
    predicted = summed.reshape(rows_here, columns, pixels)
    ratio = measured / (predicted + dark_level)
    return (predicted, ratio)


def solution(mesh):
    placed = (
        P("frames", "lenslet", None, None),
        P(("frames", "lenslet"), None, None),
        P("lenslet", None),
        P(),
        P(),
        P(),
    )
    return jax.shard_map(
        body,
        mesh=mesh,
        in_specs=placed,
        out_specs=(P(("frames", "lenslet"), None, None), P(("frames", "lenslet"), None, None)),
        check_vma=False,
    )
```

profile of v0, /device:TPU:1, one launch (start us, length us, event | category | flops | bytes accessed | tf_op | source)
XLA Modules:
  0.0 349.6 jit_solution(12887176921181222401)
XLA Ops:
  7.2 0.0 all-gather.3.cloned.1.call-start
  7.2 0.7 all-gather.3.cloned.1.call-update
  7.9 2.1 fusion.10
  10.0 4.5 %collective-permute-start = (bf16[4,2,64,400]{3,2,1,0:T(8,128)(2,1)}, bf16[4,2,64,400]{3,2,1,0:T(8,128)(2,1)S(1)}, u32[]{:S(2)}, u32[]{:S(2)}) collective-permute-start(bf16[4,2,64,400]{3,2,1,0:T(8,128)(2,1)} %get-tuple-element.2), channel_id=1, source_target_pairs={{0,1},{1,2},{2,3},{3,4},{4,5},{5,6},{6,7},{7,8},{8,9},{9,10},{10,1... | collective-permute-start | bytes 1228808 | tf_op jit(solution)/shard_map/ppermute | solution.py:12
  14.5 1.9 collective-permute-start.1
  16.5 0.8 reduce-window.8
  17.3 0.1 convert_reduce_fusion
  17.4 0.8 slice_bitcast_fusion
  18.1 0.2 add_add_fusion.1
  18.3 0.3 add.184
  18.6 0.3 add.187
  18.9 0.2 compare_select_fusion.1
  19.1 0.2 compare_and_fusion
  19.3 6.8 %broadcast_in_dim.12 = pred[1024,32,400]{2,1,0:T(32,128)(4,1)} broadcast(pred[1024,32]{1,0:T(8,128)(4,1)S(1)} %compare_and_fusion), dimensions={0,1} | broadcast | bytes 13139968 | tf_op jit(solution)/shard_map/jit(_take)/broadcast_in_dim | solution.py:22
  26.0 53.5 %broadcast_in_dim.20 = pred[16,64,12800]{2,1,0:T(32,128)(4,1)} reshape(pred[1024,32,400]{2,1,0:T(32,128)(4,1)} %broadcast_in_dim.12) | data formatting | bytes 26214400 | tf_op jit(solution)/shard_map/jit(_take)/broadcast_in_dim | solution.py:22
  79.5 0.0 collective-permute-done
  79.5 0.0 collective-permute-done.1
  79.5 8.0 %fusion.8 = bf16[4,20,68,400]{3,2,1,0:T(8,128)(2,1)} fusion(bf16[4,2,64,400]{3,2,1,0:T(8,128)(2,1)S(1)} %collective-permute-done.1, bf16[4,16,64,400]{3,2,1,0:T(8,128)(2,1)} %param.6, bf16[4,2,64,400]{3,2,1,0:T(8,128)(2,1)S(1)} %collective-permute-done), kind=kLoop, calls=%fused_computation.11 | loop fusion | flops 26112000 | bytes 8448000 | tf_op jit(solution)/shard_map/concatenate | solution.py:37
  87.6 9.2 %reshape.157 = bf16[5440,400]{1,0:T(8,128)(2,1)} reshape(bf16[4,20,68,400]{3,2,1,0:T(8,128)(2,1)} %fusion.8) | data formatting | bytes 8704000 | tf_op jit(solution)/shard_map/reshape | solution.py:40
  96.8 135.6 %gather_fusion = bf16[32768,400]{1,0:T(8,128)(2,1)} fusion(bf16[5440,400]{1,0:T(8,128)(2,1)} %reshape.157, s32[32768]{0:T(1024)S(1)} %broadcast_clamp_fusion), kind=kCustom, calls=%fused_computation | custom fusion | bytes 52559872 | tf_op jit(solution)/shard_map/jit(_take)/gather | solution.py:22
  232.4 52.4 %gather.7 = bf16[16,64,12800]{2,1,0:T(8,128)(2,1)} reshape(bf16[32768,400]{1,0:T(8,128)(2,1)} %gather_fusion) | data formatting | bytes 52428800 | tf_op jit(solution)/shard_map/jit(_take)/gather | solution.py:22
  284.8 0.0 all-gather.3.cloned.1.call-done
  284.8 16.2 %copy.11 = bf16[16,800,400]{1,0,2:T(8,128)(2,1)} copy(bf16[16,800,400]{1,2,0:T(8,128)(2,1)} %all-gather.3.cloned.1.call-done) | data formatting | bytes 20480000 | tf_op jit(solution)/shard_map/all_gather | solution.py:46
  300.9 0.0 copy-start
  301.0 0.0 copy-start.1
  301.0 18.7 %reshape.168 = bf16[12800,400,1]{0,1,2:T(8,128)(2,1)} reshape(bf16[16,800,400]{1,0,2:T(8,128)(2,1)} %copy.11) | data formatting | bytes 20480000
  319.7 0.0 copy-done
  319.7 0.0 copy-done.1
  319.7 23.0 %add_divide_fusion = (f32[16,64,400]{2,1,0:T(8,128)}, f32[16,64,400]{2,1,0:T(8,128)}) fusion(f32[16,64,400]{2,1,0:T(8,128)S(1)} %copy-done, f32[400]{0:T(512)S(1)} %copy-done.1, bf16[12800,400,1]{0,1,2:T(8,128)(2,1)} %reshape.168, pred[16,64,12800]{2,1,0:T(32,128)(4,1)} %broadcast_in_dim.20, bf16[16,64,12800]{2,1,0:T(8,128)(2,1)} %gather.7), kind=kOutput, calls=%fused_computation.12 | convolution fusion | flops 10499686400 | bytes 54478400 | tf_op jit(solution)/shard_map/dot_general | solution.py:44
  (3 shorter events, 0.0 us)
Async XLA Ops:
  7.2 277.6 %all-gather.3.cloned.1.call-start = ((), (), s32[]{:S(2)}) async-start(), calls=%async_computation | async-start | bytes 12185600 | tf_op jit(solution)/shard_map/all_gather | solution.py:46
  10.0 69.5 %collective-permute-start = (bf16[4,2,64,400]{3,2,1,0:T(8,128)(2,1)}, bf16[4,2,64,400]{3,2,1,0:T(8,128)(2,1)S(1)}, u32[]{:S(2)}, u32[]{:S(2)}) collective-permute-start(bf16[4,2,64,400]{3,2,1,0:T(8,128)(2,1)} %get-tuple-element.2), channel_id=1, source_target_pairs={{0,1},{1,2},{2,3},{3,4},{4,5},{5,6},{6,7},{7,8},{8,9},{9,10},{10,1... | collective-permute-start | bytes 1228808 | tf_op jit(solution)/shard_map/ppermute | solution.py:12
  14.5 65.0 %collective-permute-start.1 = (bf16[4,2,64,400]{3,2,1,0:T(8,128)(2,1)S(1)}, bf16[4,2,64,400]{3,2,1,0:T(8,128)(2,1)S(1)}, u32[]{:S(2)}, u32[]{:S(2)}) collective-permute-start(bf16[4,2,64,400]{3,2,1,0:T(8,128)(2,1)S(1)} %get-tuple-element.3), channel_id=1, source_target_pairs={{1,0},{2,1},{3,2},{4,3},{5,4},{6,5},{7,6},{8,7},{9,8},{10,9},{11,1... | collective-permute-start | bytes 1228808 | tf_op jit(solution)/shard_map/ppermute | solution.py:12
  300.9 18.7 %copy-start = (f32[16,64,400]{2,1,0:T(8,128)S(1)}, f32[16,64,400]{2,1,0:T(8,128)}, u32[]{:S(2)}) copy-start(f32[16,64,400]{2,1,0:T(8,128)} %param.7) | copy-start | bytes 4915204
  301.0 18.7 %copy-start.1 = (f32[400]{0:T(512)S(1)}, f32[400]{0:T(512)}, u32[]{:S(2)}) copy-start(f32[400]{0:T(512)} %param.11) | copy-start | bytes 4804
Sparse Core Ops, SparseCore 0:
  10.2 98.2 all-gather.2
where the time goes:
time: 352 us; the launch traced here: 350 us
  local copies, waits for them, and re-layouts  295 us (84%)
  matrix products  23 us (7%)
  between operations  14.1 us (4%)
  other arithmetic  10.3 us (3%)
  starting transfers between devices  6.48 us (2%)
    gather x2, local copies, waits for them, and re-layouts, gather_slabs(): taken = jnp.take(table, index.reshape(-1), axis=0)  188 us
    broadcast_in_dim x2, local copies, waits for them, and re-layouts, gather_slabs(): taken = jnp.take(table, index.reshape(-1), axis=0)  60.3 us
    dot_general x1, matrix products, body(): jnp.dot(stacked, lax.all_gather(operator_rows, 'lenslet', axis=0, tiled=T...  23 us
    unnamed x5, local copies, waits for them, and re-layouts  18.7 us
    all_gather x1, local copies, waits for them, and re-layouts, body(): lax.all_gather(operator_rows, 'lenslet', axis=0, tiled=True)  16.2 us
    reshape x1, local copies, waits for them, and re-layouts, body(): table = extended.reshape(depths * rows_ext * cols_ext, pixels)  9.23 us
    concatenate x1, other arithmetic, body(): extended = jnp.concatenate([above, volume, below], axis=1)  8.03 us
  transfers between devices with their start and end apart: 3, of which 0 were waited for; matrix products, arithmetic and copies ran while one was open for 77% of the time, Pallas kernels for 0%

commit v1 on v0

--- a/solution.py
+++ b/solution.py
@@ -4,6 +4,19 @@
 from jax.sharding import PartitionSpec as P
 
 REACH = 2
+
+
+def collect(value, axis, dim):
+    ways = lax.axis_size(axis)
+    up = [(d, (d + 1) % ways) for d in range(ways)]
+    down = [(d, (d - 1) % ways) for d in range(ways)]
+    earlier, later = ([value], [value])
+    for _ in range(ways // 2):
+        earlier.append(lax.ppermute(earlier[-1], axis, up))
+    for _ in range((ways - 1) // 2):
+        later.append(lax.ppermute(later[-1], axis, down))
+    line = jnp.concatenate([*earlier[::-1], *later[1:]], axis=dim)
+    return jnp.roll(line, (lax.axis_index(axis) - ways // 2) * value.shape[dim], axis=dim)
 
 
 def passed_along(block, axis, distance):
@@ -42,9 +55,7 @@
         table, depth_of, row_shift + REACH, col_shift, rows_here, columns, rows_ext, cols_ext
     )
     summed = jnp.dot(
-        stacked,
-        lax.all_gather(operator_rows, "lenslet", axis=0, tiled=True),
-        preferred_element_type=jnp.float32,
+        stacked, collect(operator_rows, "lenslet", 0), preferred_element_type=jnp.float32
     )
     predicted = summed.reshape(rows_here, columns, pixels)
     ratio = measured / (predicted + dark_level)

time: 352 us -> 462 us (1.31)
  waiting for transfers between devices: 0.69 us -> 90 us
  starting transfers between devices: 6.48 us -> 23.8 us
  between operations: 14.1 us -> 0.76 us
  matrix products: 23 us -> 31.4 us
    ppermute x0 -> x15, waiting for transfers between devices: none -> 90 us  [the longest x8 55.2 us: collect(): earlier.append(lax.ppermute(earlier[-1], axis, up))]
    concatenate x0 -> x1, local copies, waits for them, and re-layouts: none -> 36.9 us  [collect(): jnp.roll(line, (lax.axis_index(axis) - ways // 2) * value.shape[dim], axi...]
    unnamed x5 -> x6, local copies, waits for them, and re-layouts: 18.7 us -> 0.01 us
    ppermute x0 -> x15, starting transfers between devices: none -> 18.7 us  [the longest x8 18.7 us: collect(): earlier.append(lax.ppermute(earlier[-1], axis, up))]
    all_gather x1 -> x0, local copies, waits for them, and re-layouts: 16.2 us -> none  [body(): lax.all_gather(operator_rows, 'lenslet', axis=0, tiled=True)]
    dot_general x1, matrix products: 23 us -> 31.4 us  [body(): jnp.dot(stacked, collect(operator_rows, 'lenslet', 0), preferred_element_...]
  transfers between devices with their start and end apart: 3 -> 17, of which waited for: 0 -> 9; matrix products, arithmetic and copies ran while one was open for 77% -> 60% of each run, Pallas kernels for 0% -> 0%
where the time goes in v1:
time: 462 us; the launch traced here: 457 us
  local copies, waits for them, and re-layouts  299 us (65%)
  waiting for transfers between devices  90 us (19%)
  matrix products  31.4 us (7%)
  starting transfers between devices  23.8 us (5%)
  other arithmetic  11.9 us (3%)
    gather x2, local copies, waits for them, and re-layouts, gather_slabs(): taken = jnp.take(table, index.reshape(-1), axis=0)  189 us
    broadcast_in_dim x2, local copies, waits for them, and re-layouts, gather_slabs(): taken = jnp.take(table, index.reshape(-1), axis=0)  60.3 us
    ppermute x8, waiting for transfers between devices, collect(): earlier.append(lax.ppermute(earlier[-1], axis, up))  55.2 us
    concatenate x1, local copies, waits for them, and re-layouts, collect(): jnp.roll(line, (lax.axis_index(axis) - ways // 2) * value.shape[dim], axi...  36.9 us
    ppermute x7, waiting for transfers between devices, collect(): later.append(lax.ppermute(later[-1], axis, down))  34.8 us
    dot_general x1, matrix products, body(): jnp.dot(stacked, collect(operator_rows, 'lenslet', 0), preferred_element_...  31.4 us
    ppermute x8, starting transfers between devices, collect(): earlier.append(lax.ppermute(earlier[-1], axis, up))  18.7 us
  transfers between devices with their start and end apart: 17, of which 9 were waited for; matrix products, arithmetic and copies ran while one was open for 60% of the time, Pallas kernels for 0%

profile of v1, /device:TPU:1, one launch (start us, length us, event | category | flops | bytes accessed | tf_op | source)
XLA Modules:
  0.0 457.1 jit_solution(16951099252606722276)
XLA Ops:
  0.6 2.7 collective-permute-start.2
  3.3 16.2 %collective-permute-done.2 = bf16[800,400]{0,1:T(8,128)(2,1)S(1)} collective-permute-done((bf16[800,400]{0,1:T(8,128)(2,1)}, bf16[800,400]{0,1:T(8,128)(2,1)S(1)}, u32[]{:S(2)}, u32[]{:S(2)}) %collective-permute-start.2) | collective-permute-done | bytes 640032 | tf_op jit(solution)/shard_map/ppermute | solution.py:15
  19.5 2.4 collective-permute-start.3
  21.9 7.7 %collective-permute-done.10 = bf16[800,400]{0,1:T(8,128)(2,1)S(1)} collective-permute-done((bf16[800,400]{0,1:T(8,128)(2,1)}, bf16[800,400]{0,1:T(8,128)(2,1)S(1)}, u32[]{:S(2)}, u32[]{:S(2)}) %collective-permute-start.10) | collective-permute-done | bytes 640032 | tf_op jit(solution)/shard_map/ppermute | solution.py:17
  29.6 7.5 %collective-permute-done.3 = bf16[800,400]{0,1:T(8,128)(2,1)S(1)} collective-permute-done((bf16[800,400]{0,1:T(8,128)(2,1)S(1)}, bf16[800,400]{0,1:T(8,128)(2,1)S(1)}, u32[]{:S(2)}, u32[]{:S(2)}) %collective-permute-start.3) | collective-permute-done | bytes 640032 | tf_op jit(solution)/shard_map/ppermute | solution.py:15
  37.1 2.5 collective-permute-start.4
  39.6 8.3 %collective-permute-done.11 = bf16[800,400]{0,1:T(8,128)(2,1)S(1)} collective-permute-done((bf16[800,400]{0,1:T(8,128)(2,1)S(1)}, bf16[800,400]{0,1:T(8,128)(2,1)S(1)}, u32[]{:S(2)}, u32[]{:S(2)}) %collective-permute-start.11) | collective-permute-done | bytes 640032 | tf_op jit(solution)/shard_map/ppermute | solution.py:17
  47.9 6.8 %collective-permute-done.4 = bf16[800,400]{0,1:T(8,128)(2,1)} collective-permute-done((bf16[800,400]{0,1:T(8,128)(2,1)S(1)}, bf16[800,400]{0,1:T(8,128)(2,1)}, u32[]{:S(2)}, u32[]{:S(2)}) %collective-permute-start.4) | collective-permute-done | bytes 640032 | tf_op jit(solution)/shard_map/ppermute | solution.py:15
  54.7 2.6 collective-permute-start.5
  57.2 2.3 fusion.13
  59.5 1.9 collective-permute-start
  61.5 3.2 collective-permute-start.1
  66.4 1.9 collective-permute-start.6
  68.2 1.1 add_add_fusion.1
  69.4 1.3 add.195
  71.6 16.0 %collective-permute-done.13 = bf16[800,400]{0,1:T(8,128)(2,1)} collective-permute-done((bf16[800,400]{0,1:T(8,128)(2,1)}, bf16[800,400]{0,1:T(8,128)(2,1)}, u32[]{:S(2)}, u32[]{:S(2)}) %collective-permute-start.13) | collective-permute-done | bytes 640032 | tf_op jit(solution)/shard_map/ppermute | solution.py:17
  87.6 12.4 %collective-permute-done.6 = bf16[800,400]{0,1:T(8,128)(2,1)} collective-permute-done((bf16[800,400]{0,1:T(8,128)(2,1)}, bf16[800,400]{0,1:T(8,128)(2,1)}, u32[]{:S(2)}, u32[]{:S(2)}) %collective-permute-start.6) | collective-permute-done | bytes 640032 | tf_op jit(solution)/shard_map/ppermute | solution.py:15
  100.0 2.5 collective-permute-start.7
  102.5 1.1 compare_select_fusion.1
  103.6 2.7 collective-permute-done.14
  106.3 12.4 %collective-permute-done.7 = bf16[800,400]{0,1:T(8,128)(2,1)} collective-permute-done((bf16[800,400]{0,1:T(8,128)(2,1)}, bf16[800,400]{0,1:T(8,128)(2,1)}, u32[]{:S(2)}, u32[]{:S(2)}) %collective-permute-start.7) | collective-permute-done | bytes 640032 | tf_op jit(solution)/shard_map/ppermute | solution.py:15
  118.7 2.5 collective-permute-start.8
  121.2 1.2 compare_and_fusion
  122.5 6.7 %broadcast_in_dim.12 = pred[1024,32,400]{2,1,0:T(32,128)(4,1)} broadcast(pred[1024,32]{1,0:T(8,128)(4,1)S(1)} %compare_and_fusion), dimensions={0,1} | broadcast | bytes 13139968 | tf_op jit(solution)/shard_map/jit(_take)/broadcast_in_dim | solution.py:35
  129.2 53.5 %broadcast_in_dim.20 = pred[16,64,12800]{2,1,0:T(32,128)(4,1)} reshape(pred[1024,32,400]{2,1,0:T(32,128)(4,1)} %broadcast_in_dim.12) | data formatting | bytes 26214400 | tf_op jit(solution)/shard_map/jit(_take)/broadcast_in_dim | solution.py:35
  182.8 1.7 collective-permute-start.9
  184.5 6.7 %fusion.10 = bf16[4,20,68,400]{3,2,1,0:T(8,128)(2,1)} fusion(bf16[4,2,64,400]{3,2,1,0:T(8,128)(2,1)} %collective-permute-done.1, bf16[4,16,64,400]{3,2,1,0:T(8,128)(2,1)} %param.6, bf16[4,2,64,400]{3,2,1,0:T(8,128)(2,1)} %collective-permute-done), kind=kLoop, calls=%fused_computation.13 | loop fusion | flops 26112000 | bytes 8448000 | tf_op jit(solution)/shard_map/concatenate | solution.py:50
  191.2 9.0 %reshape.157 = bf16[5440,400]{1,0:T(8,128)(2,1)} reshape(bf16[4,20,68,400]{3,2,1,0:T(8,128)(2,1)} %fusion.10) | data formatting | bytes 8704000 | tf_op jit(solution)/shard_map/reshape | solution.py:53
  200.2 136.1 %gather_fusion = bf16[32768,400]{1,0:T(8,128)(2,1)} fusion(bf16[5440,400]{1,0:T(8,128)(2,1)} %reshape.157, s32[32768]{0:T(1024)S(1)} %broadcast_clamp_fusion), kind=kCustom, calls=%fused_computation | custom fusion | bytes 52559872 | tf_op jit(solution)/shard_map/jit(_take)/gather | solution.py:35
  336.3 52.5 %gather.7 = bf16[16,64,12800]{2,1,0:T(8,128)(2,1)} reshape(bf16[32768,400]{1,0:T(8,128)(2,1)} %gather_fusion) | data formatting | bytes 52428800 | tf_op jit(solution)/shard_map/jit(_take)/gather | solution.py:35
  388.8 36.9 %concatenate.10 = bf16[25600,400]{0,1:T(8,128)(2,1)} concatenate(bf16[800,400]{0,1:T(8,128)(2,1)} %collective-permute-done.9, bf16[800,400]{0,1:T(8,128)(2,1)} %collective-permute-done.8, bf16[800,400]{0,1:T(8,128)(2,1)} %collective-permute-done.7, bf16[800,400]{0,1:T(8,128)(2,1)} %collective-permute-done.6, bf16[800,400]{0,1:T(8,128)(2,1)} %collective-permute-done.5, ...), dimensions={0} | concatenate | bytes 40960000 | tf_op jit(solution)/shard_map/jit(_roll_dynamic)/concatenate | solution.py:19
  425.7 31.4 %add_divide_fusion = (f32[16,64,400]{2,1,0:T(8,128)}, f32[16,64,400]{2,1,0:T(8,128)}) fusion(f32[16,64,400]{2,1,0:T(8,128)} %param.7, f32[400]{0:T(512)S(1)} %copy-done.2, bf16[25600,400]{0,1:T(8,128)(2,1)} %concatenate.10, s32[]{:T(128)S(6)} %select_n.40, pred[16,64,12800]{2,1,0:T(32,128)(4,1)} %broadcast_in_dim.20, bf16[16,64,12800]{2,1,0:T(8,128)(2,1)} %gather.7), kind=kOutput, calls=%fused_computation.14 | convolution fusion | flops 10499686400 | bytes 54937156 | tf_op jit(solution)/shard_map/dot_general | solution.py:57
  (28 shorter events, 2.7 us)
Async XLA Ops:
  0.6 18.9 %collective-permute-start.2 = (bf16[800,400]{0,1:T(8,128)(2,1)}, bf16[800,400]{0,1:T(8,128)(2,1)S(1)}, u32[]{:S(2)}, u32[]{:S(2)}) collective-permute-start(bf16[800,400]{0,1:T(8,128)(2,1)} %param.8), channel_id=1, source_target_pairs={{0,1},{1,2},{2,3},{3,4},{4,5},{5,6},{6,7},{7,8},{8,9},{9,10},{10,1... | collective-permute-start | bytes 1920008 | tf_op jit(solution)/shard_map/ppermute | solution.py:15
  3.3 26.2 %collective-permute-start.10 = (bf16[800,400]{0,1:T(8,128)(2,1)}, bf16[800,400]{0,1:T(8,128)(2,1)S(1)}, u32[]{:S(2)}, u32[]{:S(2)}) collective-permute-start(bf16[800,400]{0,1:T(8,128)(2,1)} %param.8), channel_id=1, source_target_pairs={{0,15},{1,0},{2,1},{3,2},{4,3},{5,4},{6,5},{7,6},{8,7},{9,8},{10,9... | collective-permute-start | bytes 1920008 | tf_op jit(solution)/shard_map/ppermute | solution.py:17
  19.5 17.6 %collective-permute-start.3 = (bf16[800,400]{0,1:T(8,128)(2,1)S(1)}, bf16[800,400]{0,1:T(8,128)(2,1)S(1)}, u32[]{:S(2)}, u32[]{:S(2)}) collective-permute-start(bf16[800,400]{0,1:T(8,128)(2,1)S(1)} %collective-permute-done.2), channel_id=1, source_target_pairs={{0,1},{1,2},{2,3},{3,4},{4,5},{5,6},{6,7},{7,8},{8,9},{9,10},{10,1... | collective-permute-start | bytes 1920008 | tf_op jit(solution)/shard_map/ppermute | solution.py:15
  29.6 18.3 %collective-permute-start.11 = (bf16[800,400]{0,1:T(8,128)(2,1)S(1)}, bf16[800,400]{0,1:T(8,128)(2,1)S(1)}, u32[]{:S(2)}, u32[]{:S(2)}) collective-permute-start(bf16[800,400]{0,1:T(8,128)(2,1)S(1)} %collective-permute-done.10), channel_id=1, source_target_pairs={{0,15},{1,0},{2,1},{3,2},{4,3},{5,4},{6,5},{7,6},{8,7},{9,8},{10,9... | collective-permute-start | bytes 1920008 | tf_op jit(solution)/shard_map/ppermute | solution.py:17
  37.1 17.6 %collective-permute-start.4 = (bf16[800,400]{0,1:T(8,128)(2,1)S(1)}, bf16[800,400]{0,1:T(8,128)(2,1)}, u32[]{:S(2)}, u32[]{:S(2)}) collective-permute-start(bf16[800,400]{0,1:T(8,128)(2,1)S(1)} %collective-permute-done.3), channel_id=1, source_target_pairs={{0,1},{1,2},{2,3},{3,4},{4,5},{5,6},{6,7},{7,8},{8,9},{9,10},{10,1... | collective-permute-start | bytes 1920008 | tf_op jit(solution)/shard_map/ppermute | solution.py:15
  47.9 134.8 %copy-start.1 = (bf16[800,400]{0,1:T(8,128)(2,1)}, bf16[800,400]{0,1:T(8,128)(2,1)S(1)}, u32[]{:S(2)}) copy-start(bf16[800,400]{0,1:T(8,128)(2,1)S(1)} %collective-permute-done.11) | copy-start | bytes 1920004
  47.9 18.4 %collective-permute-start.12 = (bf16[800,400]{0,1:T(8,128)(2,1)S(1)}, bf16[800,400]{0,1:T(8,128)(2,1)}, u32[]{:S(2)}, u32[]{:S(2)}) collective-permute-start(bf16[800,400]{0,1:T(8,128)(2,1)S(1)} %collective-permute-done.11), channel_id=1, source_target_pairs={{0,15},{1,0},{2,1},{3,2},{4,3},{5,4},{6,5},{7,6},{8,7},{9,8},{10,9... | collective-permute-start | bytes 1920008 | tf_op jit(solution)/shard_map/ppermute | solution.py:17
  54.7 11.7 %collective-permute-start.5 = (bf16[800,400]{0,1:T(8,128)(2,1)}, bf16[800,400]{0,1:T(8,128)(2,1)}, u32[]{:S(2)}, u32[]{:S(2)}) collective-permute-start(bf16[800,400]{0,1:T(8,128)(2,1)} %collective-permute-done.4), channel_id=1, source_target_pairs={{0,1},{1,2},{2,3},{3,4},{4,5},{5,6},{6,7},{7,8},{8,9},{9,10},{10,1... | collective-permute-start | bytes 1920008 | tf_op jit(solution)/shard_map/ppermute | solution.py:15
  59.5 125.0 %collective-permute-start = (bf16[4,2,64,400]{3,2,1,0:T(8,128)(2,1)}, bf16[4,2,64,400]{3,2,1,0:T(8,128)(2,1)}, u32[]{:S(2)}, u32[]{:S(2)}) collective-permute-start(bf16[4,2,64,400]{3,2,1,0:T(8,128)(2,1)} %get-tuple-element.2), channel_id=1, source_target_pairs={{0,1},{1,2},{2,3},{3,4},{4,5},{5,6},{6,7},{7,8},{8,9},{9,10},{10,1... | collective-permute-start | bytes 1228808 | tf_op jit(solution)/shard_map/ppermute | solution.py:25
  61.5 123.0 %collective-permute-start.1 = (bf16[4,2,64,400]{3,2,1,0:T(8,128)(2,1)}, bf16[4,2,64,400]{3,2,1,0:T(8,128)(2,1)}, u32[]{:S(2)}, u32[]{:S(2)}) collective-permute-start(bf16[4,2,64,400]{3,2,1,0:T(8,128)(2,1)} %get-tuple-element.3), channel_id=1, source_target_pairs={{1,0},{2,1},{3,2},{4,3},{5,4},{6,5},{7,6},{8,7},{9,8},{10,9},{11,1... | collective-permute-start | bytes 1228808 | tf_op jit(solution)/shard_map/ppermute | solution.py:25
  66.3 21.3 %collective-permute-start.13 = (bf16[800,400]{0,1:T(8,128)(2,1)}, bf16[800,400]{0,1:T(8,128)(2,1)}, u32[]{:S(2)}, u32[]{:S(2)}) collective-permute-start(bf16[800,400]{0,1:T(8,128)(2,1)} %collective-permute-done.12), channel_id=1, source_target_pairs={{0,15},{1,0},{2,1},{3,2},{4,3},{5,4},{6,5},{7,6},{8,7},{9,8},{10,9... | collective-permute-start | bytes 1920008 | tf_op jit(solution)/shard_map/ppermute | solution.py:17
  66.4 33.7 %collective-permute-start.6 = (bf16[800,400]{0,1:T(8,128)(2,1)}, bf16[800,400]{0,1:T(8,128)(2,1)}, u32[]{:S(2)}, u32[]{:S(2)}) collective-permute-start(bf16[800,400]{0,1:T(8,128)(2,1)} %collective-permute-done.5), channel_id=1, source_target_pairs={{0,1},{1,2},{2,3},{3,4},{4,5},{5,6},{6,7},{7,8},{8,9},{9,10},{10,1... | collective-permute-start | bytes 1920008 | tf_op jit(solution)/shard_map/ppermute | solution.py:15
  87.6 18.7 %collective-permute-start.14 = (bf16[800,400]{0,1:T(8,128)(2,1)}, bf16[800,400]{0,1:T(8,128)(2,1)}, u32[]{:S(2)}, u32[]{:S(2)}) collective-permute-start(bf16[800,400]{0,1:T(8,128)(2,1)} %collective-permute-done.13), channel_id=1, source_target_pairs={{0,15},{1,0},{2,1},{3,2},{4,3},{5,4},{6,5},{7,6},{8,7},{9,8},{10,9... | collective-permute-start | bytes 1920008 | tf_op jit(solution)/shard_map/ppermute | solution.py:17
  100.0 18.7 %collective-permute-start.7 = (bf16[800,400]{0,1:T(8,128)(2,1)}, bf16[800,400]{0,1:T(8,128)(2,1)}, u32[]{:S(2)}, u32[]{:S(2)}) collective-permute-start(bf16[800,400]{0,1:T(8,128)(2,1)} %collective-permute-done.6), channel_id=1, source_target_pairs={{0,1},{1,2},{2,3},{3,4},{4,5},{5,6},{6,7},{7,8},{8,9},{9,10},{10,1... | collective-permute-start | bytes 1920008 | tf_op jit(solution)/shard_map/ppermute | solution.py:15
  106.3 76.4 %collective-permute-start.15 = (bf16[800,400]{0,1:T(8,128)(2,1)}, bf16[800,400]{0,1:T(8,128)(2,1)}, u32[]{:S(2)}, u32[]{:S(2)}) collective-permute-start(bf16[800,400]{0,1:T(8,128)(2,1)} %collective-permute-done.14), channel_id=1, source_target_pairs={{0,15},{1,0},{2,1},{3,2},{4,3},{5,4},{6,5},{7,6},{8,7},{9,8},{10,9... | collective-permute-start | bytes 1920008 | tf_op jit(solution)/shard_map/ppermute | solution.py:17
  118.7 64.1 %collective-permute-start.8 = (bf16[800,400]{0,1:T(8,128)(2,1)}, bf16[800,400]{0,1:T(8,128)(2,1)}, u32[]{:S(2)}, u32[]{:S(2)}) collective-permute-start(bf16[800,400]{0,1:T(8,128)(2,1)} %collective-permute-done.7), channel_id=1, source_target_pairs={{0,1},{1,2},{2,3},{3,4},{4,5},{5,6},{6,7},{7,8},{8,9},{9,10},{10,1... | collective-permute-start | bytes 1920008 | tf_op jit(solution)/shard_map/ppermute | solution.py:15
  182.7 206.0 %collective-permute-start.16 = (bf16[800,400]{0,1:T(8,128)(2,1)}, bf16[800,400]{0,1:T(8,128)(2,1)}, u32[]{:S(2)}, u32[]{:S(2)}) collective-permute-start(bf16[800,400]{0,1:T(8,128)(2,1)} %collective-permute-done.15), channel_id=1, source_target_pairs={{0,15},{1,0},{2,1},{3,2},{4,3},{5,4},{6,5},{7,6},{8,7},{9,8},{10,9... | collective-permute-start | bytes 1920008 | tf_op jit(solution)/shard_map/ppermute | solution.py:17
  182.8 206.0 %collective-permute-start.9 = (bf16[800,400]{0,1:T(8,128)(2,1)}, bf16[800,400]{0,1:T(8,128)(2,1)}, u32[]{:S(2)}, u32[]{:S(2)}) collective-permute-start(bf16[800,400]{0,1:T(8,128)(2,1)} %collective-permute-done.8), channel_id=1, source_target_pairs={{0,1},{1,2},{2,3},{3,4},{4,5},{5,6},{6,7},{7,8},{8,9},{9,10},{10,1... | collective-permute-start | bytes 1920008 | tf_op jit(solution)/shard_map/ppermute | solution.py:15
  336.3 52.5 %copy-start = (bf16[800,400]{0,1:T(8,128)(2,1)S(1)}, bf16[800,400]{0,1:T(8,128)(2,1)}, u32[]{:S(2)}) copy-start(bf16[800,400]{0,1:T(8,128)(2,1)} %param.8) | copy-start | bytes 1920004
  388.8 37.0 %copy-start.2 = (f32[400]{0:T(512)S(1)}, f32[400]{0:T(512)}, u32[]{:S(2)}) copy-start(f32[400]{0:T(512)} %param.11) | copy-start | bytes 4804
